TPU v7x, 256 devices: a whole 4x4x8 slice. The times are simulated.
256 devices in a mesh: pipe: 4 (over y), fsdp: 32 (over x_hi, z, core), tensor: 2 (over x_lo).
Axes of the slice: x: 4 (x_hi: 2, x_lo: 2; x = x_hi * 2 + x_lo), y: 4, z: 8, core: 2. Of those that a mesh axis runs over, the one named last changes fastest.
Arguments:
- tokens: bfloat16 [6144, 4096], P('fsdp', 'tensor'), may hold values from -8 to 8
- norm_gains: float32 [4, 4096], P('pipe'), may hold values from 0.1 to 1.9
- q_blocks: bfloat16 [4, 4, 16, 256, 256], P('pipe', None, 'tensor', 'fsdp'), may hold values from -1 to 1
- k_blocks: bfloat16 [4, 4, 16, 256, 256], P('pipe', None, 'tensor', 'fsdp'), may hold values from -1 to 1
- v_blocks: bfloat16 [4, 4, 16, 256, 256], P('pipe', None, 'tensor', 'fsdp'), may hold values from -0.1875 to 0.1875
- o_blocks: bfloat16 [4, 4, 16, 256, 256], P('pipe', 'tensor', None, 'fsdp'), may hold values from -0.1875 to 0.1875
- q_rows: int32 [4, 4, 16], P('pipe', None, 'tensor'), may hold values from 0 to 15, as said below
- k_rows: int32 [4, 4, 16], P('pipe', None, 'tensor'), may hold values from 0 to 15, as said below
- v_rows: int32 [4, 4, 16], P('pipe', None, 'tensor'), may hold values from 0 to 15, as said below
- o_rows: int32 [4, 4, 16], P('pipe', 'tensor'), may hold values from 0 to 7, as said below
- mask_blocks: int32 [96, 4, 4], P('fsdp'), may hold values from 0 to 1, as said below
Outputs:
- activations: bfloat16 [4, 6144, 4096], P('pipe', 'fsdp', 'tensor')
Inputs may be any that keep to these rules, and one draw needn't show every extreme that they name: `q_rows`: for each section and column block the 4 listed input blocks are distinct. `k_rows`: for each section and column block the 4 listed input blocks are distinct. `v_rows`: for each section and column block the 4 listed input blocks are distinct. `o_rows`: entries k and k2 with k // 2 == k2 // 2 name distinct head blocks of one column block. Every diagonal block mask_blocks[n, i, i] is 1.
All inputs are finite; a program needn't handle non-finite values.
Results may differ from a plain program's by a relative error of at most 0.017.
Values may be sent and summed in bfloat16 or wider, within the bound.
A program may use at most 64 MiB of HBM per device.

v0:
```python
import jax
import jax.numpy as jnp
from jax import lax
from jax.sharding import PartitionSpec as P

HD = 128
MBLK = 16


def from_behind(value, axis, steps):
    count = lax.axis_size(axis)
    initial, last = (max(0, -steps), min(count, count - steps))
    return lax.ppermute(value, axis, [(source, source + steps) for source in range(initial, last)])


def block_project(in_rows, blocks, pattern):
    row_count = in_rows.shape[0]
    block_width = blocks.shape[-1]
    row_blocks = in_rows.reshape(row_count, -1, block_width)
    picked = row_blocks[:, pattern]
    product = jnp.einsum("rpcb,pcbe->rce", picked, blocks, preferred_element_type=jnp.float32)
    return product.reshape(row_count, -1)


def run_layer(
    u_half, mask_now, gain_row, q_full, k_full, v_full, out_weights, q_rows, k_rows, v_rows, o_rows
):
    gathered = lax.all_gather(u_half, "tensor", axis=1, tiled=True)
    values = gathered.astype(jnp.float32)
    inv_rms = lax.rsqrt(jnp.mean(values * values, axis=-1, keepdims=True) + 1e-05)
    normed = (values * inv_rms * gain_row[None, :]).astype(jnp.bfloat16)
    queries = block_project(normed, q_full, q_rows).astype(jnp.bfloat16)
    keys_proj = block_project(normed, k_full, k_rows).astype(jnp.bfloat16)
    values_proj = block_project(normed, v_full, v_rows).astype(jnp.bfloat16)
    o_full = out_weights()
    row_count = queries.shape[0]
    head_count = queries.shape[1] // HD
    head_shape = (row_count, head_count, HD)
    scores = jnp.einsum(
        "qhd,khd->hqk",
        queries.reshape(head_shape),
        keys_proj.reshape(head_shape),
        preferred_element_type=jnp.float32,
    ) * HD ** (-0.5)
    allowed = jnp.repeat(jnp.repeat(mask_now, MBLK, axis=0), MBLK, axis=1) == 1
    scores = jnp.where(allowed[None], scores, jnp.float32(-1e30))
    row_max = jnp.max(scores, axis=-1, keepdims=True)
    exp_scores = jnp.exp(scores - row_max)
    probs = (exp_scores / jnp.sum(exp_scores, axis=-1, keepdims=True)).astype(jnp.bfloat16)
    attended = jnp.einsum(
        "hqk,khd->qhd", probs, values_proj.reshape(head_shape), preferred_element_type=jnp.float32
    )
    attended = attended.astype(jnp.bfloat16).reshape(row_count, head_count * HD)
    partial_out = block_project(attended, o_full, o_rows)
    branch = lax.psum_scatter(
        partial_out.astype(jnp.bfloat16), "tensor", scatter_dimension=1, tiled=True
    ).astype(jnp.float32)
    return (u_half.astype(jnp.float32) + branch).astype(jnp.bfloat16)


def body(
    tokens,
    norm_gains,
    q_blocks,
    k_blocks,
    v_blocks,
    o_blocks,
    q_rows,
    k_rows,
    v_rows,
    o_rows,
    mask_blocks,
):
    sections = lax.axis_size("pipe")
    segment_idx = lax.axis_index("pipe")
    micro_count = mask_blocks.shape[0]
    seq_len = tokens.shape[0] // micro_count
    half_width = tokens.shape[1]
    q_full, k_full, v_full, o_all = (
        lax.all_gather(q_blocks, "fsdp", axis=3, tiled=True),
        lax.all_gather(k_blocks, "fsdp", axis=3, tiled=True),
        lax.all_gather(v_blocks, "fsdp", axis=3, tiled=True),
        lax.all_gather(o_blocks, "fsdp", axis=3, tiled=True),
    )

    def out_weights():
        return o_all[0]

    results = jnp.zeros((micro_count * seq_len, half_width), jnp.bfloat16)
    incoming = jnp.zeros((seq_len, half_width), jnp.bfloat16)
    total_steps = micro_count + sections - 1
    for step_idx in range(total_steps):
        if step_idx < micro_count:
            fresh_rows = tokens[step_idx * seq_len : (step_idx + 1) * seq_len]
        else:
            fresh_rows = jnp.zeros_like(incoming)
        u_half = jnp.where(segment_idx == 0, fresh_rows, incoming)
        offset = step_idx - segment_idx
        slot_idx = jnp.clip(offset, 0, micro_count - 1)
        mask_now = lax.dynamic_index_in_dim(mask_blocks, slot_idx, 0, keepdims=False)
        h_half = run_layer(
            u_half,
            mask_now,
            norm_gains[0],
            q_full[0],
            k_full[0],
            v_full[0],
            out_weights,
            q_rows[0],
            k_rows[0],
            v_rows[0],
            o_rows[0],
        )
        is_valid = (offset >= 0) & (offset < micro_count)
        row_start = slot_idx * seq_len
        current = lax.dynamic_slice_in_dim(results, row_start, seq_len, 0)
        results = lax.dynamic_update_slice_in_dim(
            results, jnp.where(is_valid, h_half, current), row_start, 0
        )
        if step_idx + 1 < total_steps:
            incoming = from_behind(h_half, "pipe", 1)
    return results[None]


def solution(mesh):
    placed = (
        P("fsdp", "tensor"),
        P("pipe", None),
        P("pipe", None, "tensor", "fsdp", None),
        P("pipe", None, "tensor", "fsdp", None),
        P("pipe", None, "tensor", "fsdp", None),
        P("pipe", "tensor", None, "fsdp", None),
        P("pipe", None, "tensor"),
        P("pipe", None, "tensor"),
        P("pipe", None, "tensor"),
        P("pipe", "tensor", None),
        P("fsdp", None, None),
    )
    return jax.shard_map(
        body, mesh=mesh, in_specs=placed, out_specs=P("pipe", "fsdp", "tensor"), check_vma=False
    )
```

profile of v0, /device:TPU:1, one launch (start us, length us, event | category | flops | bytes accessed | tf_op | source)
XLA Modules:
  0.0 690.7 jit_solution(11814978129373047153)
XLA Ops:
  11.5 7.5 %all_gather.30 = bf16[64,4096]{1,0:T(8,128)(2,1)S(1)} all-gather(bf16[64,2048]{1,0:T(8,128)(2,1)S(1)} %slice_select_fusion.2), channel_id=1, replica_groups=mesh['pipe'=4,'fsdp'=32,'tensor'=2] {'tensor'}, dimensions={1}, use_global_device_ids=true | all-gather | bytes 786432 | tf_op jit(solution)/shard_map/all_gather | solution.py:28
  23.5 77.3 %all-gather.7.cloned.1.call-done = bf16[1,4,8,256,256]{4,3,2,1,0:T(8,128)(2,1)} async-done(((bf16[1,4,8,8,256]{4,3,2,1,0:T(8,128)(2,1)}), bf16[1,4,8,256,256]{4,3,2,1,0:T(8,128)(2,1)}) %all-gather.7.cloned.1.call-update) | async-done | bytes 4194320 | tf_op jit(solution)/shard_map/all_gather | solution.py:80
  104.4 82.5 %all-gather.9.cloned.1.call-done = bf16[1,4,8,256,256]{4,3,2,1,0:T(8,128)(2,1)} async-done(((bf16[1,4,8,8,256]{4,3,2,1,0:T(8,128)(2,1)}), bf16[1,4,8,256,256]{4,3,2,1,0:T(8,128)(2,1)}) %all-gather.9.cloned.1.call-update) | async-done | bytes 4194320 | tf_op jit(solution)/shard_map/all_gather | solution.py:81
  190.1 82.8 %all-gather.5.cloned.1.call-done = bf16[1,4,8,256,256]{4,3,2,1,0:T(8,128)(2,1)} async-done(((bf16[1,4,8,8,256]{4,3,2,1,0:T(8,128)(2,1)}), bf16[1,4,8,256,256]{4,3,2,1,0:T(8,128)(2,1)}) %all-gather.5.cloned.1.call-update) | async-done | bytes 4194320 | tf_op jit(solution)/shard_map/all_gather | solution.py:82
  277.8 80.9 %all-gather.11.cloned.1.call-done = bf16[1,2,16,256,256]{4,3,2,1,0:T(8,128)(2,1)} async-done(((bf16[1,2,16,8,256]{4,3,2,1,0:T(8,128)(2,1)}), bf16[1,2,16,256,256]{4,3,2,1,0:T(8,128)(2,1)}) %all-gather.11.cloned.1.call-update) | async-done | bytes 4194320 | tf_op jit(solution)/shard_map/all_gather | solution.py:83
  362.6 16.0 %reduce-scatter.7.cloned.1.call-done = bf16[64,2048]{1,0:T(8,128)(2,1)} async-done(((bf16[64,4096]{1,0:T(8,128)(2,1)}), bf16[64,2048]{1,0:T(8,128)(2,1)}) %reduce-scatter.7.cloned.1.call-update) | async-done | bytes 262160 | tf_op jit(solution)/shard_map/reduce_scatter | solution.py:55
  383.2 4.5 collective-permute-done
  388.5 6.8 all_gather.35
  398.6 3.3 fusion.261
  416.0 23.5 %reduce-scatter.9.cloned.1.call-done = bf16[64,2048]{1,0:T(8,128)(2,1)} async-done(((bf16[64,4096]{1,0:T(8,128)(2,1)}), bf16[64,2048]{1,0:T(8,128)(2,1)}) %reduce-scatter.9.cloned.1.call-update) | async-done | bytes 262160 | tf_op jit(solution)/shard_map/reduce_scatter | solution.py:55
  444.0 4.5 collective-permute-done.1
  450.3 7.0 %all_gather.36 = bf16[64,4096]{1,0:T(8,128)(2,1)S(1)} all-gather(bf16[64,2048]{1,0:T(8,128)(2,1)S(1)} %slice_select_fusion), channel_id=1, replica_groups=mesh['pipe'=4,'fsdp'=32,'tensor'=2] {'tensor'}, dimensions={1}, use_global_device_ids=true | all-gather | bytes 786432 | tf_op jit(solution)/shard_map/all_gather | solution.py:28
  460.6 3.3 fusion.264
  478.0 23.5 %reduce-scatter.11.cloned.1.call-done = bf16[64,2048]{1,0:T(8,128)(2,1)} async-done(((bf16[64,4096]{1,0:T(8,128)(2,1)}), bf16[64,2048]{1,0:T(8,128)(2,1)}) %reduce-scatter.11.cloned.1.call-update) | async-done | bytes 262160 | tf_op jit(solution)/shard_map/reduce_scatter | solution.py:55
  506.0 4.5 collective-permute-done.2
  510.6 6.9 all_gather.37
  538.2 23.4 %reduce-scatter.13.cloned.1.call-done = bf16[64,2048]{1,0:T(8,128)(2,1)} async-done(((bf16[64,4096]{1,0:T(8,128)(2,1)}), bf16[64,2048]{1,0:T(8,128)(2,1)}) %reduce-scatter.13.cloned.1.call-update) | async-done | bytes 262160 | tf_op jit(solution)/shard_map/reduce_scatter | solution.py:55
  566.1 4.5 collective-permute-done.3
  570.6 7.0 %all_gather.38 = bf16[64,4096]{1,0:T(8,128)(2,1)S(1)} all-gather(bf16[64,2048]{1,0:T(8,128)(2,1)S(1)} %broadcast_select_fusion.1), channel_id=1, replica_groups=mesh['pipe'=4,'fsdp'=32,'tensor'=2] {'tensor'}, dimensions={1}, use_global_device_ids=true | all-gather | bytes 786432 | tf_op jit(solution)/shard_map/all_gather | solution.py:28
  581.0 3.3 fusion.270
  598.4 23.6 %reduce-scatter.15.cloned.1.call-done = bf16[64,2048]{1,0:T(8,128)(2,1)} async-done(((bf16[64,4096]{1,0:T(8,128)(2,1)}), bf16[64,2048]{1,0:T(8,128)(2,1)}) %reduce-scatter.15.cloned.1.call-update) | async-done | bytes 262160 | tf_op jit(solution)/shard_map/reduce_scatter | solution.py:55
  626.5 4.5 collective-permute-done.4
  631.0 6.8 all_gather.39
  659.4 22.6 %reduce-scatter.17.cloned.1.call-done = bf16[64,2048]{1,0:T(8,128)(2,1)} async-done(((bf16[64,4096]{1,0:T(8,128)(2,1)}), bf16[64,2048]{1,0:T(8,128)(2,1)}) %reduce-scatter.17.cloned.1.call-update) | async-done | bytes 262160 | tf_op jit(solution)/shard_map/reduce_scatter | solution.py:55
  (254 shorter events, 145.2 us)
Async XLA Ops:
  6.5 13.6 %copy-start.13 = (s32[1,4,8]{2,1,0:T(4,128)S(1)}, s32[1,4,8]{2,1,0:T(4,128)}, u32[]{:S(2)}) copy-start(s32[1,4,8]{2,1,0:T(4,128)} %param.18) | copy-start | bytes 388
  6.5 94.2 %all-gather.7.cloned.1.call-start = ((), (), s32[]{:S(2)}) async-start(), calls=%async_computation.7 | async-start | bytes 4325376 | tf_op jit(solution)/shard_map/all_gather | solution.py:80
  7.3 179.6 %all-gather.9.cloned.1.call-start = ((), (), s32[]{:S(2)}) async-start(), calls=%async_computation.8 | async-start | bytes 4325376 | tf_op jit(solution)/shard_map/all_gather | solution.py:81
  8.0 264.8 %all-gather.5.cloned.1.call-start = ((), (), s32[]{:S(2)}) async-start(), calls=%async_computation.6 | async-start | bytes 4325376 | tf_op jit(solution)/shard_map/all_gather | solution.py:82
  8.7 13.9 %copy-start.12 = (s32[1,4,8]{2,1,0:T(4,128)S(1)}, s32[1,4,8]{2,1,0:T(4,128)}, u32[]{:S(2)}) copy-start(s32[1,4,8]{2,1,0:T(4,128)} %param.19) | copy-start | bytes 388
  8.8 350.0 %all-gather.11.cloned.1.call-start = ((), (), s32[]{:S(2)}) async-start(), calls=%async_computation.9 | async-start | bytes 4325376 | tf_op jit(solution)/shard_map/all_gather | solution.py:83
  9.3 369.3 %reduce-scatter.7.cloned.1.call-start = ((), (), s32[]{:S(2)}) async-start(), calls=%async_computation.10 | async-start | bytes 786432 | tf_op jit(solution)/shard_map/reduce_scatter | solution.py:55
  277.8 100.9 %copy-start.4 = (bf16[192,2048]{1,0:T(8,128)(2,1)S(1)}, bf16[192,2048]{1,0:T(8,128)(2,1)}, u32[]{:S(2)}) copy-start(bf16[192,2048]{1,0:T(8,128)(2,1)} %param.11) | copy-start | bytes 2359300
  361.7 33.8 %copy-start.11 = (f32[1,4096]{1,0:T(1,128)S(1)}, f32[1,4096]{1,0:T(1,128)}, u32[]{:S(2)}) copy-start(f32[1,4096]{1,0:T(1,128)} %param.12) | copy-start | bytes 49156
  362.6 76.9 %reduce-scatter.9.cloned.1.call-start = ((), (), s32[]{:S(2)}) async-start(), calls=%async_computation.11 | async-start | bytes 786432 | tf_op jit(solution)/shard_map/reduce_scatter | solution.py:55
  379.8 7.9 %collective-permute-start = (bf16[64,2048]{1,0:T(8,128)(2,1)S(1)}, bf16[64,2048]{1,0:T(8,128)(2,1)S(1)}, u32[]{:S(2)}, u32[]{:S(2)}) collective-permute-start(bf16[64,2048]{1,0:T(8,128)(2,1)S(1)} %get-tuple-element.14), channel_id=1, source_target_pairs={{0,64},{64,128},{128,192},{1,65},{65,129},{129,193},{2,66},{66,130... | collective-permute-start | bytes 786440 | tf_op jit(solution)/shard_map/ppermute | solution.py:13
  412.1 27.4 %copy-start.1 = (bf16[64,2048]{1,0:T(8,128)(2,1)S(1)}, bf16[64,2048]{1,0:T(8,128)(2,1)}, u32[]{:S(2)}) copy-start(bf16[64,2048]{1,0:T(8,128)(2,1)} %copy-done) | copy-start | bytes 786436
  416.0 85.5 %reduce-scatter.11.cloned.1.call-start = ((), (), s32[]{:S(2)}) async-start(), calls=%async_computation.12 | async-start | bytes 786432 | tf_op jit(solution)/shard_map/reduce_scatter | solution.py:55
  440.6 7.9 %collective-permute-start.1 = (bf16[64,2048]{1,0:T(8,128)(2,1)S(1)}, bf16[64,2048]{1,0:T(8,128)(2,1)S(1)}, u32[]{:S(2)}, u32[]{:S(2)}) collective-permute-start(bf16[64,2048]{1,0:T(8,128)(2,1)S(1)} %get-tuple-element.12), channel_id=1, source_target_pairs={{0,64},{64,128},{128,192},{1,65},{65,129},{129,193},{2,66},{66,130... | collective-permute-start | bytes 786440 | tf_op jit(solution)/shard_map/ppermute | solution.py:13
  474.1 27.4 %copy-start.3 = (bf16[64,2048]{1,0:T(8,128)(2,1)S(1)}, bf16[64,2048]{1,0:T(8,128)(2,1)}, u32[]{:S(2)}) copy-start(bf16[64,2048]{1,0:T(8,128)(2,1)} %copy-done.2) | copy-start | bytes 786436
  477.9 83.7 %reduce-scatter.13.cloned.1.call-start = ((), (), s32[]{:S(2)}) async-start(), calls=%async_computation.13 | async-start | bytes 786432 | tf_op jit(solution)/shard_map/reduce_scatter | solution.py:55
  502.6 8.0 %collective-permute-start.2 = (bf16[64,2048]{1,0:T(8,128)(2,1)S(1)}, bf16[64,2048]{1,0:T(8,128)(2,1)S(1)}, u32[]{:S(2)}, u32[]{:S(2)}) collective-permute-start(bf16[64,2048]{1,0:T(8,128)(2,1)S(1)} %get-tuple-element.10), channel_id=1, source_target_pairs={{0,64},{64,128},{128,192},{1,65},{65,129},{129,193},{2,66},{66,130... | collective-permute-start | bytes 786440 | tf_op jit(solution)/shard_map/ppermute | solution.py:13
  534.2 27.4 %copy-start.8 = (bf16[64,2048]{1,0:T(8,128)(2,1)S(1)}, bf16[64,2048]{1,0:T(8,128)(2,1)}, u32[]{:S(2)}) copy-start(bf16[64,2048]{1,0:T(8,128)(2,1)} %copy-done.7) | copy-start | bytes 786436
  538.1 83.9 %reduce-scatter.15.cloned.1.call-start = ((), (), s32[]{:S(2)}) async-start(), calls=%async_computation.14 | async-start | bytes 786432 | tf_op jit(solution)/shard_map/reduce_scatter | solution.py:55
  562.7 7.9 %collective-permute-start.3 = (bf16[64,2048]{1,0:T(8,128)(2,1)S(1)}, bf16[64,2048]{1,0:T(8,128)(2,1)S(1)}, u32[]{:S(2)}, u32[]{:S(2)}) collective-permute-start(bf16[64,2048]{1,0:T(8,128)(2,1)S(1)} %get-tuple-element.8), channel_id=1, source_target_pairs={{0,64},{64,128},{128,192},{1,65},{65,129},{129,193},{2,66},{66,130... | collective-permute-start | bytes 786440 | tf_op jit(solution)/shard_map/ppermute | solution.py:13
  594.5 27.5 %copy-start.10 = (bf16[64,2048]{1,0:T(8,128)(2,1)S(1)}, bf16[64,2048]{1,0:T(8,128)(2,1)}, u32[]{:S(2)}) copy-start(bf16[64,2048]{1,0:T(8,128)(2,1)} %copy-done.9) | copy-start | bytes 786436
  598.4 83.7 %reduce-scatter.17.cloned.1.call-start = ((), (), s32[]{:S(2)}) async-start(), calls=%async_computation.15 | async-start | bytes 786432 | tf_op jit(solution)/shard_map/reduce_scatter | solution.py:55
  623.1 7.9 %collective-permute-start.4 = (bf16[64,2048]{1,0:T(8,128)(2,1)S(1)}, bf16[64,2048]{1,0:T(8,128)(2,1)S(1)}, u32[]{:S(2)}, u32[]{:S(2)}) collective-permute-start(bf16[64,2048]{1,0:T(8,128)(2,1)S(1)} %get-tuple-element.6), channel_id=1, source_target_pairs={{0,64},{64,128},{128,192},{1,65},{65,129},{129,193},{2,66},{66,130... | collective-permute-start | bytes 786440 | tf_op jit(solution)/shard_map/ppermute | solution.py:13
  654.7 27.4 %copy-start.6 = (bf16[64,2048]{1,0:T(8,128)(2,1)S(1)}, bf16[64,2048]{1,0:T(8,128)(2,1)}, u32[]{:S(2)}) copy-start(bf16[64,2048]{1,0:T(8,128)(2,1)} %copy-done.5) | copy-start | bytes 786436
  (7 other events, 41.3 us)
Sparse Core Ops, SparseCore 0:
  9.9 90.8 all-gather.6
  103.3 83.4 all-gather.8
  189.4 83.4 all-gather.4
  275.3 83.4 all-gather.10
  362.7 15.8 reduce-scatter.6
  416.1 23.3 reduce-scatter.8
  478.1 23.3 reduce-scatter.10
  538.2 23.3 reduce-scatter.12
  598.5 23.4 reduce-scatter.14
  658.7 23.3 reduce-scatter.16
where the time goes:
time: 692 us; the launch traced here: 691 us
  waiting for transfers between devices  481 us (70%)
  matrix products  82.2 us (12%)
  blocking collectives  42 us (6%)
  local copies, waits for them, and re-layouts  40.1 us (6%)
  starting transfers between devices  16 us (2%)
  between operations  14.9 us (2%)
  other arithmetic  14.1 us (2%)
    reduce_scatter x6, waiting for transfers between devices, run_layer(): lax.psum_scatter(partial_out.astype(jnp.bfloat16), 'tensor', scatter_dime...  133 us
    all_gather x1, waiting for transfers between devices, body(): lax.all_gather(v_blocks, 'fsdp', axis=3, tiled=True)  82.8 us
    all_gather x1, waiting for transfers between devices, body(): lax.all_gather(k_blocks, 'fsdp', axis=3, tiled=True)  82.5 us
    all_gather x1, waiting for transfers between devices, body(): lax.all_gather(o_blocks, 'fsdp', axis=3, tiled=True)  80.9 us
    all_gather x1, waiting for transfers between devices, body(): lax.all_gather(q_blocks, 'fsdp', axis=3, tiled=True)  77.3 us
    dot_general x24, matrix products, block_project(): jnp.einsum('rpcb,pcbe->rce', picked, blocks, preferred_element_type=jnp.f...  73.8 us
    all_gather x6, blocking collectives, run_layer(): gathered = lax.all_gather(u_half, 'tensor', axis=1, tiled=True)  42 us
    ppermute x5, waiting for transfers between devices, from_behind(): lax.ppermute(value, axis, [(source, source + steps) for source in range(i...  22.6 us
  transfers between devices with their start and end apart: 15, of which 15 were waited for; matrix products, arithmetic and copies ran while one was open for 3% of the time, Pallas kernels for 0%

commit v1 on v0

--- a/solution.py
+++ b/solution.py
@@ -76,10 +76,18 @@
     micro_count = mask_blocks.shape[0]
     seq_len = tokens.shape[0] // micro_count
     half_width = tokens.shape[1]
+
+    def process_the_target(z_in, net_axis):
+        queue = []
+        for _ in range(lax.axis_size(net_axis)):
+            queue.append(z_in)
+        tile_out = jnp.concatenate(lax.all_to_all(jnp.stack(queue, axis=0), net_axis, 0, 0), axis=3)
+        return tile_out
+
     q_full, k_full, v_full, o_all = (
         lax.all_gather(q_blocks, "fsdp", axis=3, tiled=True),
         lax.all_gather(k_blocks, "fsdp", axis=3, tiled=True),
-        lax.all_gather(v_blocks, "fsdp", axis=3, tiled=True),
+        process_the_target(v_blocks, net_axis="fsdp"),
         lax.all_gather(o_blocks, "fsdp", axis=3, tiled=True),
     )
 

time: 692 us -> 649 us (0.938)
  waiting for transfers between devices: 481 us -> 415 us
  starting transfers between devices: 16 us -> 28.9 us
  blocking collectives: 42 us -> 52.6 us
    all_gather x1 -> x0, waiting for transfers between devices: 82.8 us -> none  [body(): lax.all_gather(v_blocks, 'fsdp', axis=3, tiled=True)]
    all_gather x1, waiting for transfers between devices: 77.3 us -> 96 us  [body(): lax.all_gather(q_blocks, 'fsdp', axis=3, tiled=True)]
    all_to_all x0 -> x1, starting transfers between devices: none -> 12.8 us  [process_the_target(): lax.all_to_all(jnp.stack(queue, axis=0), net_axis, 0, 0)]
    all_gather x6, blocking collectives: 42 us -> 52.6 us  [run_layer(): gathered = lax.all_gather(u_half, 'tensor', axis=1, tiled=True)]
  transfers between devices with their start and end apart: 15 -> 15, of which waited for: 15 -> 14; matrix products, arithmetic and copies ran while one was open for 3% -> 3% of each run, Pallas kernels for 0% -> 0%
where the time goes in v1:
time: 649 us; the launch traced here: 647 us
  waiting for transfers between devices  415 us (64%)
  matrix products  80.9 us (12%)
  blocking collectives  52.6 us (8%)
  local copies, waits for them, and re-layouts  44.2 us (7%)
  starting transfers between devices  28.9 us (4%)
  between operations  14.6 us (2%)
  other arithmetic  11.6 us (2%)
    reduce_scatter x6, waiting for transfers between devices, run_layer(): lax.psum_scatter(partial_out.astype(jnp.bfloat16), 'tensor', scatter_dime...  133 us
    all_gather x1, waiting for transfers between devices, body(): lax.all_gather(q_blocks, 'fsdp', axis=3, tiled=True)  96 us
    all_gather x1, waiting for transfers between devices, body(): lax.all_gather(k_blocks, 'fsdp', axis=3, tiled=True)  83.7 us
    all_gather x1, waiting for transfers between devices, body(): lax.all_gather(o_blocks, 'fsdp', axis=3, tiled=True)  77.7 us
    dot_general x24, matrix products, block_project(): jnp.einsum('rpcb,pcbe->rce', picked, blocks, preferred_element_type=jnp.f...  72.5 us
    all_gather x6, blocking collectives, run_layer(): gathered = lax.all_gather(u_half, 'tensor', axis=1, tiled=True)  52.6 us
    ppermute x5, waiting for transfers between devices, from_behind(): lax.ppermute(value, axis, [(source, source + steps) for source in range(i...  22.4 us
    gather x24, local copies, waits for them, and re-layouts, block_project(): picked = row_blocks[:, pattern]  20.7 us
  transfers between devices with their start and end apart: 15, of which 14 were waited for; matrix products, arithmetic and copies ran while one was open for 3% of the time, Pallas kernels for 0%

profile of v1, /device:TPU:1, one launch (start us, length us, event | category | flops | bytes accessed | tf_op | source)
XLA Modules:
  0.0 647.4 jit_solution(1813750320073196486)
XLA Ops:
  8.0 3.4 stack.2
  11.4 12.8 %all-to-all-start = ((bf16[32,1,4,8,8,256]{5,4,3,2,1,0:T(8,128)(2,1)}), bf16[32,1,4,8,8,256]{5,4,3,2,1,0:T(8,128)(2,1)}, u32[]{:S(2)}, u32[]{:S(2)}) async-start(bf16[32,1,4,8,8,256]{5,4,3,2,1,0:T(8,128)(2,1)} %stack.2), calls=%async_computation | async-start | bytes 8388608 | tf_op jit(solution)/shard_map/all_to_all | solution.py:84
  25.3 18.2 %all_gather.27 = bf16[64,4096]{1,0:T(8,128)(2,1)S(1)} all-gather(bf16[64,2048]{1,0:T(8,128)(2,1)S(1)} %slice_select_fusion.2), channel_id=1, replica_groups=mesh['pipe'=4,'fsdp'=32,'tensor'=2] {'tensor'}, dimensions={1}, use_global_device_ids=true | all-gather | bytes 786432 | tf_op jit(solution)/shard_map/all_gather | solution.py:28
  47.3 96.0 %all-gather.4.cloned.1.call-done = bf16[1,4,8,256,256]{4,3,2,1,0:T(8,128)(2,1)} async-done(((bf16[1,4,8,8,256]{4,3,2,1,0:T(8,128)(2,1)}), bf16[1,4,8,256,256]{4,3,2,1,0:T(8,128)(2,1)}) %all-gather.4.cloned.1.call-update) | async-done | bytes 4194320 | tf_op jit(solution)/shard_map/all_gather | solution.py:88
  147.2 83.7 %all-gather.6.cloned.1.call-done = bf16[1,4,8,256,256]{4,3,2,1,0:T(8,128)(2,1)} async-done(((bf16[1,4,8,8,256]{4,3,2,1,0:T(8,128)(2,1)}), bf16[1,4,8,256,256]{4,3,2,1,0:T(8,128)(2,1)}) %all-gather.6.cloned.1.call-update) | async-done | bytes 4194320 | tf_op jit(solution)/shard_map/all_gather | solution.py:89
  239.3 77.7 %all-gather.8.cloned.1.call-done = bf16[1,2,16,256,256]{4,3,2,1,0:T(8,128)(2,1)} async-done(((bf16[1,2,16,8,256]{4,3,2,1,0:T(8,128)(2,1)}), bf16[1,2,16,256,256]{4,3,2,1,0:T(8,128)(2,1)}) %all-gather.8.cloned.1.call-update) | async-done | bytes 4194320 | tf_op jit(solution)/shard_map/all_gather | solution.py:91
  320.9 16.0 %reduce-scatter.7.cloned.1.call-done = bf16[64,2048]{1,0:T(8,128)(2,1)} async-done(((bf16[64,4096]{1,0:T(8,128)(2,1)}), bf16[64,2048]{1,0:T(8,128)(2,1)}) %reduce-scatter.7.cloned.1.call-update) | async-done | bytes 262160 | tf_op jit(solution)/shard_map/reduce_scatter | solution.py:55
  341.4 4.5 collective-permute-done
  346.7 6.8 %all_gather.31 = bf16[64,4096]{1,0:T(8,128)(2,1)S(1)} all-gather(bf16[64,2048]{1,0:T(8,128)(2,1)S(1)} %slice_select_fusion.1), channel_id=1, replica_groups=mesh['pipe'=4,'fsdp'=32,'tensor'=2] {'tensor'}, dimensions={1}, use_global_device_ids=true | all-gather | bytes 786432 | tf_op jit(solution)/shard_map/all_gather | solution.py:28
  374.0 23.5 %reduce-scatter.9.cloned.1.call-done = bf16[64,2048]{1,0:T(8,128)(2,1)} async-done(((bf16[64,4096]{1,0:T(8,128)(2,1)}), bf16[64,2048]{1,0:T(8,128)(2,1)}) %reduce-scatter.9.cloned.1.call-update) | async-done | bytes 262160 | tf_op jit(solution)/shard_map/reduce_scatter | solution.py:55
  398.6 3.3 collective-permute-start.1
  402.2 4.3 collective-permute-done.1
  408.3 6.8 %all_gather.32 = bf16[64,4096]{1,0:T(8,128)(2,1)S(1)} all-gather(bf16[64,2048]{1,0:T(8,128)(2,1)S(1)} %slice_select_fusion), channel_id=1, replica_groups=mesh['pipe'=4,'fsdp'=32,'tensor'=2] {'tensor'}, dimensions={1}, use_global_device_ids=true | all-gather | bytes 786432 | tf_op jit(solution)/shard_map/all_gather | solution.py:28
  435.6 23.5 %reduce-scatter.11.cloned.1.call-done = bf16[64,2048]{1,0:T(8,128)(2,1)} async-done(((bf16[64,4096]{1,0:T(8,128)(2,1)}), bf16[64,2048]{1,0:T(8,128)(2,1)}) %reduce-scatter.11.cloned.1.call-update) | async-done | bytes 262160 | tf_op jit(solution)/shard_map/reduce_scatter | solution.py:55
  463.6 4.5 collective-permute-done.2
  468.2 6.8 %all_gather.33 = bf16[64,4096]{1,0:T(8,128)(2,1)S(1)} all-gather(bf16[64,2048]{1,0:T(8,128)(2,1)S(1)} %broadcast_select_fusion.2), channel_id=1, replica_groups=mesh['pipe'=4,'fsdp'=32,'tensor'=2] {'tensor'}, dimensions={1}, use_global_device_ids=true | all-gather | bytes 786432 | tf_op jit(solution)/shard_map/all_gather | solution.py:28
  495.5 23.5 %reduce-scatter.13.cloned.1.call-done = bf16[64,2048]{1,0:T(8,128)(2,1)} async-done(((bf16[64,4096]{1,0:T(8,128)(2,1)}), bf16[64,2048]{1,0:T(8,128)(2,1)}) %reduce-scatter.13.cloned.1.call-update) | async-done | bytes 262160 | tf_op jit(solution)/shard_map/reduce_scatter | solution.py:55
  520.1 3.1 collective-permute-start.3
  523.5 4.5 collective-permute-done.3
  528.1 7.1 %all_gather.34 = bf16[64,4096]{1,0:T(8,128)(2,1)S(1)} all-gather(bf16[64,2048]{1,0:T(8,128)(2,1)S(1)} %broadcast_select_fusion.1), channel_id=1, replica_groups=mesh['pipe'=4,'fsdp'=32,'tensor'=2] {'tensor'}, dimensions={1}, use_global_device_ids=true | all-gather | bytes 786432 | tf_op jit(solution)/shard_map/all_gather | solution.py:28
  555.7 23.5 %reduce-scatter.15.cloned.1.call-done = bf16[64,2048]{1,0:T(8,128)(2,1)} async-done(((bf16[64,4096]{1,0:T(8,128)(2,1)}), bf16[64,2048]{1,0:T(8,128)(2,1)}) %reduce-scatter.15.cloned.1.call-update) | async-done | bytes 262160 | tf_op jit(solution)/shard_map/reduce_scatter | solution.py:55
  583.7 4.5 collective-permute-done.4
  588.3 6.8 %all_gather.35 = bf16[64,4096]{1,0:T(8,128)(2,1)S(1)} all-gather(bf16[64,2048]{1,0:T(8,128)(2,1)S(1)} %broadcast_select_fusion), channel_id=1, replica_groups=mesh['pipe'=4,'fsdp'=32,'tensor'=2] {'tensor'}, dimensions={1}, use_global_device_ids=true | all-gather | bytes 786432 | tf_op jit(solution)/shard_map/all_gather | solution.py:28
  616.5 22.6 %reduce-scatter.17.cloned.1.call-done = bf16[64,2048]{1,0:T(8,128)(2,1)} async-done(((bf16[64,4096]{1,0:T(8,128)(2,1)}), bf16[64,2048]{1,0:T(8,128)(2,1)}) %reduce-scatter.17.cloned.1.call-update) | async-done | bytes 262160 | tf_op jit(solution)/shard_map/reduce_scatter | solution.py:55
  (270 shorter events, 145.2 us)
Async XLA Ops:
  6.5 136.7 %all-gather.4.cloned.1.call-start = ((), (), s32[]{:S(2)}) async-start(), calls=%async_computation.7 | async-start | bytes 4325376 | tf_op jit(solution)/shard_map/all_gather | solution.py:88
  7.3 223.7 %all-gather.6.cloned.1.call-start = ((), (), s32[]{:S(2)}) async-start(), calls=%async_computation.8 | async-start | bytes 4325376 | tf_op jit(solution)/shard_map/all_gather | solution.py:89
  11.4 32.4 %copy-start.17 = (f32[1,4096]{1,0:T(1,128)S(1)}, f32[1,4096]{1,0:T(1,128)}, u32[]{:S(2)}) copy-start(f32[1,4096]{1,0:T(1,128)} %param.12) | copy-start | bytes 49156
  11.4 32.7 %copy-start.21 = (s32[1,4,8]{2,1,0:T(4,128)S(1)}, s32[1,4,8]{2,1,0:T(4,128)}, u32[]{:S(2)}) copy-start(s32[1,4,8]{2,1,0:T(4,128)} %param.18) | copy-start | bytes 388
  11.4 32.7 %copy-start.22 = (s32[1,4,8]{2,1,0:T(4,128)S(1)}, s32[1,4,8]{2,1,0:T(4,128)}, u32[]{:S(2)}) copy-start(s32[1,4,8]{2,1,0:T(4,128)} %param.17) | copy-start | bytes 388
  11.4 222.8 %all-to-all-start = ((bf16[32,1,4,8,8,256]{5,4,3,2,1,0:T(8,128)(2,1)}), bf16[32,1,4,8,8,256]{5,4,3,2,1,0:T(8,128)(2,1)}, u32[]{:S(2)}, u32[]{:S(2)}) async-start(bf16[32,1,4,8,8,256]{5,4,3,2,1,0:T(8,128)(2,1)} %stack.2), calls=%async_computation | async-start | bytes 8388608 | tf_op jit(solution)/shard_map/all_to_all | solution.py:84
  24.2 292.8 %all-gather.8.cloned.1.call-start = ((), (), s32[]{:S(2)}) async-start(), calls=%async_computation.9 | async-start | bytes 4325376 | tf_op jit(solution)/shard_map/all_gather | solution.py:91
  24.9 311.9 %reduce-scatter.7.cloned.1.call-start = ((), (), s32[]{:S(2)}) async-start(), calls=%async_computation.10 | async-start | bytes 786432 | tf_op jit(solution)/shard_map/reduce_scatter | solution.py:55
  146.3 87.9 %copy-start.7 = (bf16[32,64,256]{2,1,0:T(8,128)(2,1)S(1)}, bf16[32,64,256]{2,1,0:T(8,128)(2,1)}, u32[]{:S(2)}) copy-start(bf16[32,64,256]{2,1,0:T(8,128)(2,1)} %gather_fusion) | copy-start | bytes 3145732
  320.8 76.7 %reduce-scatter.9.cloned.1.call-start = ((), (), s32[]{:S(2)}) async-start(), calls=%async_computation.11 | async-start | bytes 786432 | tf_op jit(solution)/shard_map/reduce_scatter | solution.py:55
  338.0 7.9 %collective-permute-start = (bf16[64,2048]{1,0:T(8,128)(2,1)S(1)}, bf16[64,2048]{1,0:T(8,128)(2,1)S(1)}, u32[]{:S(2)}, u32[]{:S(2)}) collective-permute-start(bf16[64,2048]{1,0:T(8,128)(2,1)S(1)} %get-tuple-element.14), channel_id=1, source_target_pairs={{0,64},{64,128},{128,192},{1,65},{65,129},{129,193},{2,66},{66,130... | collective-permute-start | bytes 786440 | tf_op jit(solution)/shard_map/ppermute | solution.py:13
  370.1 27.4 %copy-start.1 = (bf16[64,2048]{1,0:T(8,128)(2,1)S(1)}, bf16[64,2048]{1,0:T(8,128)(2,1)}, u32[]{:S(2)}) copy-start(bf16[64,2048]{1,0:T(8,128)(2,1)} %copy-done) | copy-start | bytes 786436
  374.0 85.2 %reduce-scatter.11.cloned.1.call-start = ((), (), s32[]{:S(2)}) async-start(), calls=%async_computation.12 | async-start | bytes 786432 | tf_op jit(solution)/shard_map/reduce_scatter | solution.py:55
  398.6 7.9 %collective-permute-start.1 = (bf16[64,2048]{1,0:T(8,128)(2,1)S(1)}, bf16[64,2048]{1,0:T(8,128)(2,1)S(1)}, u32[]{:S(2)}, u32[]{:S(2)}) collective-permute-start(bf16[64,2048]{1,0:T(8,128)(2,1)S(1)} %get-tuple-element.12), channel_id=1, source_target_pairs={{0,64},{64,128},{128,192},{1,65},{65,129},{129,193},{2,66},{66,130... | collective-permute-start | bytes 786440 | tf_op jit(solution)/shard_map/ppermute | solution.py:13
  431.7 27.4 %copy-start.3 = (bf16[64,2048]{1,0:T(8,128)(2,1)S(1)}, bf16[64,2048]{1,0:T(8,128)(2,1)}, u32[]{:S(2)}) copy-start(bf16[64,2048]{1,0:T(8,128)(2,1)} %copy-done.2) | copy-start | bytes 786436
  435.6 83.4 %reduce-scatter.13.cloned.1.call-start = ((), (), s32[]{:S(2)}) async-start(), calls=%async_computation.13 | async-start | bytes 786432 | tf_op jit(solution)/shard_map/reduce_scatter | solution.py:55
  460.2 7.9 %collective-permute-start.2 = (bf16[64,2048]{1,0:T(8,128)(2,1)S(1)}, bf16[64,2048]{1,0:T(8,128)(2,1)S(1)}, u32[]{:S(2)}, u32[]{:S(2)}) collective-permute-start(bf16[64,2048]{1,0:T(8,128)(2,1)S(1)} %get-tuple-element.10), channel_id=1, source_target_pairs={{0,64},{64,128},{128,192},{1,65},{65,129},{129,193},{2,66},{66,130... | collective-permute-start | bytes 786440 | tf_op jit(solution)/shard_map/ppermute | solution.py:13
  491.6 27.4 %copy-start.14 = (bf16[64,2048]{1,0:T(8,128)(2,1)S(1)}, bf16[64,2048]{1,0:T(8,128)(2,1)}, u32[]{:S(2)}) copy-start(bf16[64,2048]{1,0:T(8,128)(2,1)} %copy-done.13) | copy-start | bytes 786436
  495.5 83.7 %reduce-scatter.15.cloned.1.call-start = ((), (), s32[]{:S(2)}) async-start(), calls=%async_computation.14 | async-start | bytes 786432 | tf_op jit(solution)/shard_map/reduce_scatter | solution.py:55
  520.1 8.0 %collective-permute-start.3 = (bf16[64,2048]{1,0:T(8,128)(2,1)S(1)}, bf16[64,2048]{1,0:T(8,128)(2,1)S(1)}, u32[]{:S(2)}, u32[]{:S(2)}) collective-permute-start(bf16[64,2048]{1,0:T(8,128)(2,1)S(1)} %get-tuple-element.8), channel_id=1, source_target_pairs={{0,64},{64,128},{128,192},{1,65},{65,129},{129,193},{2,66},{66,130... | collective-permute-start | bytes 786440 | tf_op jit(solution)/shard_map/ppermute | solution.py:13
  551.8 27.4 %copy-start.16 = (bf16[64,2048]{1,0:T(8,128)(2,1)S(1)}, bf16[64,2048]{1,0:T(8,128)(2,1)}, u32[]{:S(2)}) copy-start(bf16[64,2048]{1,0:T(8,128)(2,1)} %copy-done.15) | copy-start | bytes 786436
  555.7 83.5 %reduce-scatter.17.cloned.1.call-start = ((), (), s32[]{:S(2)}) async-start(), calls=%async_computation.15 | async-start | bytes 786432 | tf_op jit(solution)/shard_map/reduce_scatter | solution.py:55
  580.3 7.9 %collective-permute-start.4 = (bf16[64,2048]{1,0:T(8,128)(2,1)S(1)}, bf16[64,2048]{1,0:T(8,128)(2,1)S(1)}, u32[]{:S(2)}, u32[]{:S(2)}) collective-permute-start(bf16[64,2048]{1,0:T(8,128)(2,1)S(1)} %get-tuple-element.6), channel_id=1, source_target_pairs={{0,64},{64,128},{128,192},{1,65},{65,129},{129,193},{2,66},{66,130... | collective-permute-start | bytes 786440 | tf_op jit(solution)/shard_map/ppermute | solution.py:13
  611.7 27.4 %copy-start.6 = (bf16[64,2048]{1,0:T(8,128)(2,1)S(1)}, bf16[64,2048]{1,0:T(8,128)(2,1)}, u32[]{:S(2)}) copy-start(bf16[64,2048]{1,0:T(8,128)(2,1)} %copy-done.5) | copy-start | bytes 786436
  (15 other events, 103.2 us)
Sparse Core Ops, SparseCore 0:
  9.9 133.3 all-gather.3
  145.8 85.0 all-gather.5
  233.5 83.4 all-gather.7
  320.9 15.8 reduce-scatter.6
  374.1 23.3 reduce-scatter.8
  435.7 23.3 reduce-scatter.10
  495.6 23.3 reduce-scatter.12
  555.8 23.3 reduce-scatter.14
  615.7 23.3 reduce-scatter.16
